TPU v7x, 32 devices: a whole 2x2x4 slice. The times are simulated.
32 devices in a mesh: dom: 32 (over z, y, x, core).
Axes of the slice: x: 2, y: 2, z: 4, core: 2. Of those that a mesh axis runs over, the one named last changes fastest.
Arguments:
- features: bfloat16 [64, 262144], P(None, 'dom'), may hold values from -6 to 6
- cheb_weight: bfloat16 [4, 64, 64], replicated, may hold values from -0.375 to 0.375
- lap_tiles: bfloat16 [2048, 3, 128, 128], P('dom'), may hold values from -0.25 to 0.25
- col_index: int32 [2048, 3], P('dom'), may hold values from 0 to 63
- cross_tiles: bfloat16 [32, 5, 2, 128, 128], P('dom'), may hold values from -0.25 to 0.25
- send_index: int32 [32, 5, 2], P('dom'), may hold values from 0 to 63
- row_index: int32 [32, 5, 2], P('dom'), may hold values from 0 to 63
- pair_on: int32 [32, 5], P('dom'), may hold values 0 or 1
- blk_live: int32 [32], P('dom'), may hold values from 1 to 64, 1536 in all
- cotangent: bfloat16 [64, 262144], P(None, 'dom'), may hold values from -6 to 6
Outputs:
- conv_out: bfloat16 [64, 262144], P(None, 'dom')
- grad_x: bfloat16 [64, 262144], P(None, 'dom')
- grad_w: float32 [4, 64, 64], replicated
Inputs may be any that keep to these rules, and one draw needn't show every extreme that they name: `blk_live`: the counts sum to 1536 and the largest is exactly 64.
All inputs are finite; a program needn't handle non-finite values. No bound on the sum of `pair_on` or of `blk_live` on one device may be relied on, other than what follows from the above.
Results may differ from a plain program's by a relative error of at most 0.0059.
Values may be sent and summed in bfloat16 or wider, within the bound.
No kernel may reach another device: no remote copies, remote signals or barrier semaphores. Data moves between devices by JAX's collectives and lax.ppermute only.
A program may use at most 128 MiB of HBM per device.

v0:
```python
import jax
import jax.numpy as jnp
from jax import lax
from jax.sharding import PartitionSpec as P


def from_partner(block, axis, bit):
    count = lax.axis_size(axis)
    route = []
    for low in range(count):
        high = low | 1 << bit
        if high != low and high < count:
            route += [(low, high), (high, low)]
    return lax.ppermute(block, axis, route)


def local(
    features,
    cheb_weight,
    lap_tiles,
    col_index,
    cross_tiles,
    send_index,
    row_index,
    pair_on,
    blk_live,
    cotangent,
):
    channels = features.shape[0]
    block_count = lap_tiles.shape[0]
    block_size = lap_tiles.shape[2]
    rounds = cross_tiles.shape[1]
    live_blocks = blk_live[0]
    mask_half = (jnp.arange(block_count) < live_blocks).astype(jnp.bfloat16)[None, :, None]
    mask_full = mask_half.astype(jnp.float32)
    send_rows = send_index[0] % live_blocks
    recv_rows = row_index[0] % live_blocks
    switch = pair_on[0].astype(jnp.float32)
    coupling = cross_tiles[0]

    def apply_forward(values):
        gathered = jnp.take(values, col_index, axis=1)
        summed = jnp.einsum(
            "inab,finb->fia", lap_tiles, gathered, preferred_element_type=jnp.float32
        )
        for level in range(rounds):
            outgoing = jnp.take(values, send_rows[level], axis=1)
            incoming = from_partner(outgoing, "dom", level)
            product = jnp.einsum(
                "hab,fhb->fha", coupling[level], incoming, preferred_element_type=jnp.float32
            )
            summed = summed.at[:, recv_rows[level]].add(switch[level] * product)
        return summed

    def local_adjoint(values):
        terms = jnp.einsum("inab,fia->finb", lap_tiles, values, preferred_element_type=jnp.float32)
        return (
            jnp.zeros((channels, block_count, block_size), jnp.float32).at[:, col_index].add(terms)
        )

    flagged = coupling * pair_on[0].astype(jnp.bfloat16)[:, None, None, None]
    copies = [from_partner(flagged[level], "dom", level) for level in range(rounds)]

    def apply_adjoint(values):
        summed = local_adjoint(values)
        for level in range(rounds):
            slices = jnp.take(values, recv_rows[level], axis=1)
            incoming = from_partner(slices, "dom", level)
            contrib = jnp.einsum(
                "hab,fha->fhb", copies[level], incoming, preferred_element_type=jnp.float32
            )
            summed = summed.at[:, send_rows[level]].add(contrib)
        return summed

    zeroth = features.reshape(channels, block_count, block_size) * mask_half
    first = (apply_forward(zeroth) * mask_full).astype(jnp.bfloat16)
    second = ((2.0 * apply_forward(first) - zeroth.astype(jnp.float32)) * mask_full).astype(
        jnp.bfloat16
    )
    third = ((2.0 * apply_forward(second) - first.astype(jnp.float32)) * mask_full).astype(
        jnp.bfloat16
    )
    orders = jnp.stack([zeroth, first, second, third])
    output = (
        jnp.einsum("kfg,kfib->gib", cheb_weight, orders, preferred_element_type=jnp.float32)
        * mask_full
    )
    conv_out = output.astype(jnp.bfloat16).reshape(channels, block_count * block_size)
    upstream = cotangent.reshape(channels, block_count, block_size) * mask_half
    weight_terms = jnp.einsum("kfib,gib->kfg", orders, upstream, preferred_element_type=jnp.float32)
    grad_w = lax.psum(weight_terms, "dom")
    lifted = jnp.einsum("kfg,gib->kfib", cheb_weight, upstream, preferred_element_type=jnp.float32)
    back_third = (lifted[3] * mask_full).astype(jnp.bfloat16)
    adjoint_two = lifted[2] + 2.0 * apply_adjoint(back_third)
    back_second = (adjoint_two * mask_full).astype(jnp.bfloat16)
    adjoint_one = lifted[1] + 2.0 * apply_adjoint(back_second) - back_third.astype(jnp.float32)
    back_first = (adjoint_one * mask_full).astype(jnp.bfloat16)
    adjoint_zero = lifted[0] + apply_adjoint(back_first) - back_second.astype(jnp.float32)
    grad_x = (
        (adjoint_zero * mask_full).astype(jnp.bfloat16).reshape(channels, block_count * block_size)
    )
    return (conv_out, grad_x, grad_w)


def solution(mesh):
    in_specs = (
        P(None, "dom"),
        P(),
        P("dom", None, None, None),
        P("dom", None),
        P("dom", None, None, None, None),
        P("dom", None, None),
        P("dom", None, None),
        P("dom", None),
        P("dom"),
        P(None, "dom"),
    )
    out_specs = (P(None, "dom"), P(None, "dom"), P())
    return jax.shard_map(local, mesh=mesh, in_specs=in_specs, out_specs=out_specs, check_vma=False)
```

profile of v0, /device:TPU:0, one launch (start us, length us, event | category | flops | bytes accessed | tf_op | source)
XLA Modules:
  0.0 540.3 jit_solution(13784177287233342524)
XLA Ops:
  12.2 3.2 copy-done.3
  20.1 3.0 collective-permute-start.17
  57.3 3.2 slice_bitcast_fusion.3
  62.1 6.7 %fusion.42 = f32[64,64,3,128]{3,1,2,0:T(8,128)} fusion(bf16[64,3,128,128]{3,2,1,0:T(8,128)(2,1)} %param.16, bf16[64,64,128]{2,0,1:T(8,128)(2,1)S(1)} %fusion.13), kind=kOutput, calls=%fused_computation.133 | convolution fusion | flops 402653184 | bytes 13631488 | tf_op jit(solution)/shard_map/inab,fia->finb/dot_general | solution.py:56
  73.0 2.7 gather_fusion
  86.8 2.6 copy_multiply_fusion
  91.5 7.0 %fusion.22 = f32[64,64,128]{2,0,1:T(8,128)} fusion(bf16[64,3,128,128]{3,2,1,0:T(8,128)(2,1)} %param.16, bf16[64,3,64,128]{3,2,1,0:T(8,128)(2,1)S(1)} %bitcast.374, pred[64,3]{1,0:T(8,128)(4,1)S(1)} %copy.20), kind=kOutput, calls=%fused_computation.99 | convolution fusion | flops 404226048 | bytes 11534528 | tf_op jit(solution)/shard_map/inab,finb->fia/dot_general | solution.py:43
  102.2 20.1 %scatter_fusion.15 = f32[64,64,128]{2,0,1:T(8,128)S(1)} fusion(f32[64,64,128]{2,0,1:T(8,128)S(1)} %broadcast.220.clone, s32[192]{0:T(256)S(1)} %reshape.935, f32[192,64,128]{2,1,0:T(8,128)} %bitcast.367), kind=kCustom, calls=%fused_computation.48 | custom fusion | flops 1572864 | bytes 18875136 | tf_op jit(solution)/shard_map/scatter-add | solution.py:58
  134.9 2.9 collective-permute-start.4
  157.9 3.0 collective-permute-start.23
  177.8 6.7 %fusion.40 = f32[64,64,3,128]{3,1,2,0:T(8,128)} fusion(bf16[64,3,128,128]{3,2,1,0:T(8,128)(2,1)} %param.16, bf16[64,64,128]{2,0,1:T(8,128)(2,1)S(1)} %fusion.16), kind=kOutput, calls=%fused_computation.131 | convolution fusion | flops 402653184 | bytes 13631488 | tf_op jit(solution)/shard_map/inab,fia->finb/dot_general | solution.py:56
  202.4 2.9 collective-permute-start.29
  205.5 20.0 %scatter_fusion.21 = f32[64,64,128]{2,0,1:T(8,128)S(1)} fusion(f32[64,64,128]{2,0,1:T(8,128)S(1)} %broadcast.220, s32[192]{0:T(256)S(1)} %reshape.935, f32[192,64,128]{2,1,0:T(8,128)} %bitcast.368), kind=kCustom, calls=%fused_computation.54 | custom fusion | flops 1572864 | bytes 18875136 | tf_op jit(solution)/shard_map/scatter-add | solution.py:58
  246.0 5.7 %fusion.20 = (bf16[64,64,128]{2,0,1:T(8,128)(2,1)S(1)}, bf16[64,64,128]{2,0,1:T(8,128)(2,1)}) fusion(f32[4,64,64,128]{3,1,2,0:T(8,128)} %copy-done.3, f32[64,64,128]{2,0,1:T(8,128)} %scatter_fusion.26, f32[64]{0:T(128)} %copy-done.32, f32[64,64,128]{2,0,1:T(8,128)} %scatter_fusion.4), kind=kLoop, calls=%fused_computation.91 | loop fusion | flops 5242880 | bytes 10486016 | tf_op jit(solution)/shard_map/convert_element_type | solution.py:97
  252.7 3.9 fusion.38
  266.2 4.0 gather_fusion.6
  287.3 8.1 %fusion.25 = f32[64,64,128]{2,0,1:T(8,128)} fusion(bf16[64,3,128,128]{3,2,1,0:T(8,128)(2,1)} %param.16, bf16[64,3,64,128]{3,2,1,0:T(8,128)(2,1)} %bitcast.373, pred[64,3]{1,0:T(8,128)(4,1)S(1)} %copy.20), kind=kOutput, calls=%fused_computation.100 | convolution fusion | flops 404226048 | bytes 11534528 | tf_op jit(solution)/shard_map/inab,finb->fia/dot_general | solution.py:43
  298.9 20.0 %scatter_fusion.27 = f32[64,64,128]{2,0,1:T(8,128)S(1)} fusion(f32[64,64,128]{2,0,1:T(8,128)S(1)} %copy-done.1, s32[192]{0:T(256)S(1)} %reshape.935, f32[192,64,128]{2,1,0:T(8,128)} %bitcast.366), kind=kCustom, calls=%fused_computation.60 | custom fusion | flops 1572864 | bytes 18875136 | tf_op jit(solution)/shard_map/scatter-add | solution.py:58
  329.6 2.9 collective-permute-start.9
  359.0 4.2 fusion.36
  363.3 4.0 gather_fusion.12
  372.0 8.1 %fusion.28 = f32[64,64,128]{2,0,1:T(8,128)} fusion(bf16[64,3,128,128]{3,2,1,0:T(8,128)(2,1)} %param.16, bf16[64,3,64,128]{3,2,1,0:T(8,128)(2,1)} %bitcast.375, pred[64,3]{1,0:T(8,128)(4,1)S(1)} %copy.20), kind=kOutput, calls=%fused_computation.101 | convolution fusion | flops 404226048 | bytes 11534528 | tf_op jit(solution)/shard_map/inab,finb->fia/dot_general | solution.py:43
  405.4 2.6 fusion.34
  409.2 122.6 %all-reduce.2.cloned.1.call-done = f32[4,64,64]{2,1,0:T(8,128)} async-done(((f32[4,64,64]{2,1,0:T(8,128)}), f32[4,64,64]{2,1,0:T(8,128)}) %all-reduce.2.cloned.1.call-update) | async-done | bytes 65552 | tf_op jit(solution)/shard_map/psum | solution.py:91
  (424 shorter events, 254.5 us)
Async XLA Ops:
  7.2 524.7 %all-reduce.2.cloned.1.call-start = ((), (), s32[]{:S(2)}) async-start(), calls=%async_computation | async-start | bytes 262144 | tf_op jit(solution)/shard_map/psum | solution.py:91
  17.0 137.2 %collective-permute-start.15 = (bf16[64,2,128]{2,0,1:T(8,128)(2,1)}, bf16[64,2,128]{2,0,1:T(8,128)(2,1)}, u32[]{:S(2)}, u32[]{:S(2)}) collective-permute-start(bf16[64,2,128]{2,0,1:T(8,128)(2,1)} %select_bitcast_fusion.14), channel_id=1, source_target_pairs={{0,1},{1,0},{2,3},{3,2},{4,5},{5,4},{6,7},{7,6},{8,9},{9,8},{10,11... | collective-permute-start | bytes 98312 | tf_op jit(solution)/shard_map/ppermute | solution.py:14
  18.8 135.5 %collective-permute-start.16 = (bf16[2,128,128]{2,1,0:T(8,128)(2,1)}, bf16[2,128,128]{2,1,0:T(8,128)(2,1)S(1)}, u32[]{:S(2)}, u32[]{:S(2)}) collective-permute-start(bf16[2,128,128]{2,1,0:T(8,128)(2,1)} %get-tuple-element.19), channel_id=1, source_target_pairs={{0,1},{1,0},{2,3},{3,2},{4,5},{5,4},{6,7},{7,6},{8,9},{9,8},{10,11... | collective-permute-start | bytes 196616 | tf_op jit(solution)/shard_map/ppermute | solution.py:14
  20.1 137.7 %collective-permute-start.17 = (bf16[64,2,128]{2,0,1:T(8,128)(2,1)}, bf16[64,2,128]{2,0,1:T(8,128)(2,1)}, u32[]{:S(2)}, u32[]{:S(2)}) collective-permute-start(bf16[64,2,128]{2,0,1:T(8,128)(2,1)} %select_bitcast_fusion.13), channel_id=1, source_target_pairs={{0,2},{2,0},{1,3},{3,1},{4,6},{6,4},{5,7},{7,5},{8,10},{10,8},{9,1... | collective-permute-start | bytes 98312 | tf_op jit(solution)/shard_map/ppermute | solution.py:14
  23.1 134.8 %collective-permute-start.18 = (bf16[2,128,128]{2,1,0:T(8,128)(2,1)}, bf16[2,128,128]{2,1,0:T(8,128)(2,1)}, u32[]{:S(2)}, u32[]{:S(2)}) collective-permute-start(bf16[2,128,128]{2,1,0:T(8,128)(2,1)} %get-tuple-element.18), channel_id=1, source_target_pairs={{0,2},{2,0},{1,3},{3,1},{4,6},{6,4},{5,7},{7,5},{8,10},{10,8},{9,1... | collective-permute-start | bytes 196616 | tf_op jit(solution)/shard_map/ppermute | solution.py:14
  28.6 93.7 %collective-permute-start = (bf16[64,2,128]{2,0,1:T(8,128)(2,1)}, bf16[64,2,128]{2,0,1:T(8,128)(2,1)}, u32[]{:S(2)}, u32[]{:S(2)}) collective-permute-start(bf16[64,2,128]{2,0,1:T(8,128)(2,1)} %select_bitcast_fusion.29), channel_id=1, source_target_pairs={{0,1},{1,0},{2,3},{3,2},{4,5},{5,4},{6,7},{7,6},{8,9},{9,8},{10,11... | collective-permute-start | bytes 98312 | tf_op jit(solution)/shard_map/ppermute | solution.py:14
  140.0 22.5 %collective-permute-start.19 = (bf16[64,2,128]{2,0,1:T(8,128)(2,1)}, bf16[64,2,128]{2,0,1:T(8,128)(2,1)}, u32[]{:S(2)}, u32[]{:S(2)}) collective-permute-start(bf16[64,2,128]{2,0,1:T(8,128)(2,1)} %select_bitcast_fusion.12), channel_id=1, source_target_pairs={{0,4},{4,0},{1,5},{5,1},{2,6},{6,2},{3,7},{7,3},{8,12},{12,8},{9,1... | collective-permute-start | bytes 98312 | tf_op jit(solution)/shard_map/ppermute | solution.py:14
  157.9 13.8 %collective-permute-start.23 = (bf16[64,2,128]{2,0,1:T(8,128)(2,1)}, bf16[64,2,128]{2,0,1:T(8,128)(2,1)}, u32[]{:S(2)}, u32[]{:S(2)}) collective-permute-start(bf16[64,2,128]{2,0,1:T(8,128)(2,1)} %select_bitcast_fusion.10), channel_id=1, source_target_pairs={{0,16},{16,0},{1,17},{17,1},{2,18},{18,2},{3,19},{19,3},{4,20},{20... | collective-permute-start | bytes 98312 | tf_op jit(solution)/shard_map/ppermute | solution.py:14
  194.7 32.1 %collective-permute-start.25 = (bf16[64,2,128]{2,0,1:T(8,128)(2,1)}, bf16[64,2,128]{2,0,1:T(8,128)(2,1)}, u32[]{:S(2)}, u32[]{:S(2)}) collective-permute-start(bf16[64,2,128]{2,0,1:T(8,128)(2,1)} %select_bitcast_fusion.9), channel_id=1, source_target_pairs={{0,1},{1,0},{2,3},{3,2},{4,5},{5,4},{6,7},{7,6},{8,9},{9,8},{10,11... | collective-permute-start | bytes 98312 | tf_op jit(solution)/shard_map/ppermute | solution.py:14
  195.4 33.1 %collective-permute-start.26 = (bf16[64,2,128]{2,0,1:T(8,128)(2,1)}, bf16[64,2,128]{2,0,1:T(8,128)(2,1)}, u32[]{:S(2)}, u32[]{:S(2)}) collective-permute-start(bf16[64,2,128]{2,0,1:T(8,128)(2,1)} %select_bitcast_fusion.8), channel_id=1, source_target_pairs={{0,2},{2,0},{1,3},{3,1},{4,6},{6,4},{5,7},{7,5},{8,10},{10,8},{9,1... | collective-permute-start | bytes 98312 | tf_op jit(solution)/shard_map/ppermute | solution.py:14
  197.9 32.2 %collective-permute-start.27 = (bf16[64,2,128]{2,0,1:T(8,128)(2,1)}, bf16[64,2,128]{2,0,1:T(8,128)(2,1)}, u32[]{:S(2)}, u32[]{:S(2)}) collective-permute-start(bf16[64,2,128]{2,0,1:T(8,128)(2,1)} %select_bitcast_fusion.7), channel_id=1, source_target_pairs={{0,4},{4,0},{1,5},{5,1},{2,6},{6,2},{3,7},{7,3},{8,12},{12,8},{9,1... | collective-permute-start | bytes 98312 | tf_op jit(solution)/shard_map/ppermute | solution.py:14
  200.1 31.7 %collective-permute-start.28 = (bf16[64,2,128]{2,0,1:T(8,128)(2,1)}, bf16[64,2,128]{2,0,1:T(8,128)(2,1)}, u32[]{:S(2)}, u32[]{:S(2)}) collective-permute-start(bf16[64,2,128]{2,0,1:T(8,128)(2,1)} %select_bitcast_fusion.6), channel_id=1, source_target_pairs={{0,8},{8,0},{1,9},{9,1},{2,10},{10,2},{3,11},{11,3},{4,12},{12,4},... | collective-permute-start | bytes 98312 | tf_op jit(solution)/shard_map/ppermute | solution.py:14
  202.4 39.8 %collective-permute-start.29 = (bf16[64,2,128]{2,0,1:T(8,128)(2,1)}, bf16[64,2,128]{2,0,1:T(8,128)(2,1)}, u32[]{:S(2)}, u32[]{:S(2)}) collective-permute-start(bf16[64,2,128]{2,0,1:T(8,128)(2,1)} %select_bitcast_fusion.5), channel_id=1, source_target_pairs={{0,16},{16,0},{1,17},{17,1},{2,18},{18,2},{3,19},{19,3},{4,20},{20... | collective-permute-start | bytes 98312 | tf_op jit(solution)/shard_map/ppermute | solution.py:14
  283.3 35.5 %collective-permute-start.30 = (bf16[64,2,128]{2,0,1:T(8,128)(2,1)}, bf16[64,2,128]{2,0,1:T(8,128)(2,1)}, u32[]{:S(2)}, u32[]{:S(2)}) collective-permute-start(bf16[64,2,128]{2,0,1:T(8,128)(2,1)} %select_bitcast_fusion.4), channel_id=1, source_target_pairs={{0,1},{1,0},{2,3},{3,2},{4,5},{5,4},{6,7},{7,6},{8,9},{9,8},{10,11... | collective-permute-start | bytes 98312 | tf_op jit(solution)/shard_map/ppermute | solution.py:14
  284.0 36.4 %collective-permute-start.31 = (bf16[64,2,128]{2,0,1:T(8,128)(2,1)}, bf16[64,2,128]{2,0,1:T(8,128)(2,1)}, u32[]{:S(2)}, u32[]{:S(2)}) collective-permute-start(bf16[64,2,128]{2,0,1:T(8,128)(2,1)} %select_bitcast_fusion.3), channel_id=1, source_target_pairs={{0,2},{2,0},{1,3},{3,1},{4,6},{6,4},{5,7},{7,5},{8,10},{10,8},{9,1... | collective-permute-start | bytes 98312 | tf_op jit(solution)/shard_map/ppermute | solution.py:14
  285.1 38.1 %collective-permute-start.32 = (bf16[64,2,128]{2,0,1:T(8,128)(2,1)}, bf16[64,2,128]{2,0,1:T(8,128)(2,1)}, u32[]{:S(2)}, u32[]{:S(2)}) collective-permute-start(bf16[64,2,128]{2,0,1:T(8,128)(2,1)} %select_bitcast_fusion.2), channel_id=1, source_target_pairs={{0,4},{4,0},{1,5},{5,1},{2,6},{6,2},{3,7},{7,3},{8,12},{12,8},{9,1... | collective-permute-start | bytes 98312 | tf_op jit(solution)/shard_map/ppermute | solution.py:14
  286.3 40.1 %collective-permute-start.33 = (bf16[64,2,128]{2,0,1:T(8,128)(2,1)}, bf16[64,2,128]{2,0,1:T(8,128)(2,1)}, u32[]{:S(2)}, u32[]{:S(2)}) collective-permute-start(bf16[64,2,128]{2,0,1:T(8,128)(2,1)} %select_bitcast_fusion.1), channel_id=1, source_target_pairs={{0,8},{8,0},{1,9},{9,1},{2,10},{10,2},{3,11},{11,3},{4,12},{12,4},... | collective-permute-start | bytes 98312 | tf_op jit(solution)/shard_map/ppermute | solution.py:14
  287.2 42.4 %collective-permute-start.34 = (bf16[64,2,128]{2,0,1:T(8,128)(2,1)}, bf16[64,2,128]{2,0,1:T(8,128)(2,1)}, u32[]{:S(2)}, u32[]{:S(2)}) collective-permute-start(bf16[64,2,128]{2,0,1:T(8,128)(2,1)} %select_bitcast_fusion), channel_id=1, source_target_pairs={{0,16},{16,0},{1,17},{17,1},{2,18},{18,2},{3,19},{19,3},{4,20},{20... | collective-permute-start | bytes 98312 | tf_op jit(solution)/shard_map/ppermute | solution.py:14
  318.8 15.3 %collective-permute-start.5 = (bf16[64,2,128]{2,0,1:T(8,128)(2,1)}, bf16[64,2,128]{2,0,1:T(8,128)(2,1)S(1)}, u32[]{:S(2)}, u32[]{:S(2)}) collective-permute-start(bf16[64,2,128]{2,0,1:T(8,128)(2,1)} %select_bitcast_fusion.24), channel_id=1, source_target_pairs={{0,1},{1,0},{2,3},{3,2},{4,5},{5,4},{6,7},{7,6},{8,9},{9,8},{10,11... | collective-permute-start | bytes 98312 | tf_op jit(solution)/shard_map/ppermute | solution.py:14
  320.4 15.1 %collective-permute-start.6 = (bf16[64,2,128]{2,0,1:T(8,128)(2,1)}, bf16[64,2,128]{2,0,1:T(8,128)(2,1)S(1)}, u32[]{:S(2)}, u32[]{:S(2)}) collective-permute-start(bf16[64,2,128]{2,0,1:T(8,128)(2,1)} %select_bitcast_fusion.23), channel_id=1, source_target_pairs={{0,2},{2,0},{1,3},{3,1},{4,6},{6,4},{5,7},{7,5},{8,10},{10,8},{9,1... | collective-permute-start | bytes 98312 | tf_op jit(solution)/shard_map/ppermute | solution.py:14
  323.3 13.7 %collective-permute-start.7 = (bf16[64,2,128]{2,0,1:T(8,128)(2,1)}, bf16[64,2,128]{2,0,1:T(8,128)(2,1)S(1)}, u32[]{:S(2)}, u32[]{:S(2)}) collective-permute-start(bf16[64,2,128]{2,0,1:T(8,128)(2,1)} %select_bitcast_fusion.22), channel_id=1, source_target_pairs={{0,4},{4,0},{1,5},{5,1},{2,6},{6,2},{3,7},{7,3},{8,12},{12,8},{9,1... | collective-permute-start | bytes 98312 | tf_op jit(solution)/shard_map/ppermute | solution.py:14
  326.4 11.9 %collective-permute-start.8 = (bf16[64,2,128]{2,0,1:T(8,128)(2,1)}, bf16[64,2,128]{2,0,1:T(8,128)(2,1)S(1)}, u32[]{:S(2)}, u32[]{:S(2)}) collective-permute-start(bf16[64,2,128]{2,0,1:T(8,128)(2,1)} %select_bitcast_fusion.21), channel_id=1, source_target_pairs={{0,8},{8,0},{1,9},{9,1},{2,10},{10,2},{3,11},{11,3},{4,12},{12,4},... | collective-permute-start | bytes 98312 | tf_op jit(solution)/shard_map/ppermute | solution.py:14
  329.6 25.8 %collective-permute-start.9 = (bf16[64,2,128]{2,0,1:T(8,128)(2,1)}, bf16[64,2,128]{2,0,1:T(8,128)(2,1)}, u32[]{:S(2)}, u32[]{:S(2)}) collective-permute-start(bf16[64,2,128]{2,0,1:T(8,128)(2,1)} %select_bitcast_fusion.20), channel_id=1, source_target_pairs={{0,16},{16,0},{1,17},{17,1},{2,18},{18,2},{3,19},{19,3},{4,20},{20... | collective-permute-start | bytes 98312 | tf_op jit(solution)/shard_map/ppermute | solution.py:14
  382.4 14.5 %collective-permute-start.14 = (bf16[64,2,128]{2,0,1:T(8,128)(2,1)}, bf16[64,2,128]{2,0,1:T(8,128)(2,1)}, u32[]{:S(2)}, u32[]{:S(2)}) collective-permute-start(bf16[64,2,128]{2,0,1:T(8,128)(2,1)} %select_bitcast_fusion.15), channel_id=1, source_target_pairs={{0,16},{16,0},{1,17},{17,1},{2,18},{18,2},{3,19},{19,3},{4,20},{20... | collective-permute-start | bytes 98312 | tf_op jit(solution)/shard_map/ppermute | solution.py:14
  (97 other events, 853.4 us)
Sparse Core Ops, SparseCore 0:
  405.5 126.2 all-reduce.1
where the time goes:
time: 546 us; the launch traced here: 540 us
  other arithmetic  191 us (35%)
  waiting for transfers between devices  125 us (23%)
  matrix products  91 us (17%)
  local copies, waits for them, and re-layouts  80.2 us (15%)
  starting transfers between devices  37.6 us (7%)
  between operations  15.7 us (3%)
    psum x1, waiting for transfers between devices, local(): grad_w = lax.psum(weight_terms, 'dom')  123 us
    scatter-add x3, other arithmetic, local_adjoint(): jnp.zeros((channels, block_count, block_size), jnp.float32).at[:, col_index]  60 us
    ppermute x35, starting transfers between devices, from_partner(): return lax.ppermute(block, axis, route)  37.5 us
    scatter-add x15, other arithmetic, apply_forward(): summed = summed.at[:, recv_rows[level]].add(switch[level] * product)  32.2 us
    scatter-add x15, other arithmetic, apply_adjoint(): summed = summed.at[:, send_rows[level]].add(contrib)  25.6 us
    gather x15, local copies, waits for them, and re-layouts, apply_adjoint(): slices = jnp.take(values, recv_rows[level], axis=1)  23.7 us
    gather x15, local copies, waits for them, and re-layouts, apply_forward(): outgoing = jnp.take(values, send_rows[level], axis=1)  23.4 us
    dot_general x3, matrix products, apply_forward(): jnp.einsum('inab,finb->fia', lap_tiles, gathered, preferred_element_type=...  23.2 us
  transfers between devices with their start and end apart: 36, of which 5 were waited for; matrix products, arithmetic and copies ran while one was open for 46% of the time, Pallas kernels for 0%

commit v1 on v0

--- a/solution.py
+++ b/solution.py
@@ -88,7 +88,8 @@
     conv_out = output.astype(jnp.bfloat16).reshape(channels, block_count * block_size)
     upstream = cotangent.reshape(channels, block_count, block_size) * mask_half
     weight_terms = jnp.einsum("kfib,gib->kfg", orders, upstream, preferred_element_type=jnp.float32)
-    grad_w = lax.psum(weight_terms, "dom")
+    terms_2 = lax.all_gather(weight_terms, "dom")
+    grad_w = jnp.sum(terms_2, axis=0)
     lifted = jnp.einsum("kfg,gib->kfib", cheb_weight, upstream, preferred_element_type=jnp.float32)
     back_third = (lifted[3] * mask_full).astype(jnp.bfloat16)
     adjoint_two = lifted[2] + 2.0 * apply_adjoint(back_third)

time: 546 us -> 485 us (0.89)
  waiting for transfers between devices: 125 us -> 61.5 us
    psum x1 -> x0, waiting for transfers between devices: 123 us -> none  [local(): grad_w = lax.psum(weight_terms, 'dom')]
    all_gather x0 -> x1, waiting for transfers between devices: none -> 57.7 us  [local(): terms_2 = lax.all_gather(weight_terms, 'dom')]
    unnamed x172 -> x171, local copies, waits for them, and re-layouts: 11.3 us -> 9.72 us
  transfers between devices with their start and end apart: 36 -> 36, of which waited for: 5 -> 6; matrix products, arithmetic and copies ran while one was open for 46% -> 52% of each run, Pallas kernels for 0% -> 0%
where the time goes in v1:
time: 485 us; the launch traced here: 479 us
  other arithmetic  194 us (40%)
  matrix products  89.5 us (18%)
  local copies, waits for them, and re-layouts  80.6 us (17%)
  waiting for transfers between devices  61.5 us (13%)
  starting transfers between devices  37.5 us (8%)
  between operations  15.8 us (3%)
    scatter-add x3, other arithmetic, local_adjoint(): jnp.zeros((channels, block_count, block_size), jnp.float32).at[:, col_index]  60 us
    all_gather x1, waiting for transfers between devices, local(): terms_2 = lax.all_gather(weight_terms, 'dom')  57.7 us
    ppermute x35, starting transfers between devices, from_partner(): return lax.ppermute(block, axis, route)  37.5 us
    scatter-add x15, other arithmetic, apply_forward(): summed = summed.at[:, recv_rows[level]].add(switch[level] * product)  32.4 us
    scatter-add x15, other arithmetic, apply_adjoint(): summed = summed.at[:, send_rows[level]].add(contrib)  25.6 us
    gather x15, local copies, waits for them, and re-layouts, apply_forward(): outgoing = jnp.take(values, send_rows[level], axis=1)  24 us
    gather x15, local copies, waits for them, and re-layouts, apply_adjoint(): slices = jnp.take(values, recv_rows[level], axis=1)  23.7 us
    dot_general x3, matrix products, apply_forward(): jnp.einsum('inab,finb->fia', lap_tiles, gathered, preferred_element_type=...  23.1 us
  transfers between devices with their start and end apart: 36, of which 6 were waited for; matrix products, arithmetic and copies ran while one was open for 52% of the time, Pallas kernels for 0%

profile of v1, /device:TPU:0, one launch (start us, length us, event | category | flops | bytes accessed | tf_op | source)
XLA Modules:
  0.0 478.8 jit_solution(9509345949319660239)
XLA Ops:
  12.2 3.2 copy-done.3
  20.1 3.0 collective-permute-start.17
  57.3 3.2 slice_bitcast_fusion.3
  62.1 6.7 %fusion.42 = f32[64,64,3,128]{3,1,2,0:T(8,128)} fusion(bf16[64,3,128,128]{3,2,1,0:T(8,128)(2,1)} %param.16, bf16[64,64,128]{2,0,1:T(8,128)(2,1)S(1)} %fusion.13), kind=kOutput, calls=%fused_computation.133 | convolution fusion | flops 402653184 | bytes 13631488 | tf_op jit(solution)/shard_map/inab,fia->finb/dot_general | solution.py:56
  73.0 2.7 gather_fusion
  86.8 2.6 copy_multiply_fusion
  91.5 7.0 %fusion.22 = f32[64,64,128]{2,0,1:T(8,128)} fusion(bf16[64,3,128,128]{3,2,1,0:T(8,128)(2,1)} %param.16, bf16[64,3,64,128]{3,2,1,0:T(8,128)(2,1)S(1)} %bitcast.375, pred[64,3]{1,0:T(8,128)(4,1)S(1)} %copy.35), kind=kOutput, calls=%fused_computation.99 | convolution fusion | flops 404226048 | bytes 11534528 | tf_op jit(solution)/shard_map/inab,finb->fia/dot_general | solution.py:43
  102.2 20.1 %scatter_fusion.15 = f32[64,64,128]{2,0,1:T(8,128)S(1)} fusion(f32[64,64,128]{2,0,1:T(8,128)S(1)} %broadcast.220.clone, s32[192]{0:T(256)S(1)} %reshape.936, f32[192,64,128]{2,1,0:T(8,128)} %bitcast.368), kind=kCustom, calls=%fused_computation.48 | custom fusion | flops 1572864 | bytes 18875136 | tf_op jit(solution)/shard_map/scatter-add | solution.py:58
  134.9 2.9 collective-permute-start.4
  157.9 3.0 collective-permute-start.23
  177.8 6.7 %fusion.40 = f32[64,64,3,128]{3,1,2,0:T(8,128)} fusion(bf16[64,3,128,128]{3,2,1,0:T(8,128)(2,1)} %param.16, bf16[64,64,128]{2,0,1:T(8,128)(2,1)S(1)} %fusion.16), kind=kOutput, calls=%fused_computation.131 | convolution fusion | flops 402653184 | bytes 13631488 | tf_op jit(solution)/shard_map/inab,fia->finb/dot_general | solution.py:56
  202.4 2.9 collective-permute-start.29
  205.5 20.0 %scatter_fusion.21 = f32[64,64,128]{2,0,1:T(8,128)S(1)} fusion(f32[64,64,128]{2,0,1:T(8,128)S(1)} %broadcast.220, s32[192]{0:T(256)S(1)} %reshape.936, f32[192,64,128]{2,1,0:T(8,128)} %bitcast.369), kind=kCustom, calls=%fused_computation.54 | custom fusion | flops 1572864 | bytes 18875136 | tf_op jit(solution)/shard_map/scatter-add | solution.py:58
  246.0 5.7 %fusion.20 = (bf16[64,64,128]{2,0,1:T(8,128)(2,1)S(1)}, bf16[64,64,128]{2,0,1:T(8,128)(2,1)}) fusion(f32[4,64,64,128]{3,1,2,0:T(8,128)} %copy-done.3, f32[64,64,128]{2,0,1:T(8,128)} %scatter_fusion.26, f32[64]{0:T(128)} %copy-done.34, f32[64,64,128]{2,0,1:T(8,128)} %scatter_fusion.4), kind=kLoop, calls=%fused_computation.91 | loop fusion | flops 5242880 | bytes 10486016 | tf_op jit(solution)/shard_map/convert_element_type | solution.py:98
  252.7 3.9 fusion.38
  266.2 4.0 gather_fusion.6
  287.3 8.1 %fusion.25 = f32[64,64,128]{2,0,1:T(8,128)} fusion(bf16[64,3,128,128]{3,2,1,0:T(8,128)(2,1)} %param.16, bf16[64,3,64,128]{3,2,1,0:T(8,128)(2,1)} %bitcast.374, pred[64,3]{1,0:T(8,128)(4,1)S(1)} %copy.35), kind=kOutput, calls=%fused_computation.100 | convolution fusion | flops 404226048 | bytes 11534528 | tf_op jit(solution)/shard_map/inab,finb->fia/dot_general | solution.py:43
  298.9 20.0 %scatter_fusion.27 = f32[64,64,128]{2,0,1:T(8,128)S(1)} fusion(f32[64,64,128]{2,0,1:T(8,128)S(1)} %copy-done.1, s32[192]{0:T(256)S(1)} %reshape.936, f32[192,64,128]{2,1,0:T(8,128)} %bitcast.367), kind=kCustom, calls=%fused_computation.60 | custom fusion | flops 1572864 | bytes 18875136 | tf_op jit(solution)/shard_map/scatter-add | solution.py:58
  329.6 2.9 collective-permute-start.9
  359.0 4.2 fusion.36
  363.3 4.0 gather_fusion.12
  372.6 8.0 %fusion.28 = f32[64,64,128]{2,0,1:T(8,128)} fusion(bf16[64,3,128,128]{3,2,1,0:T(8,128)(2,1)} %param.16, bf16[64,3,64,128]{3,2,1,0:T(8,128)(2,1)} %bitcast.376, pred[64,3]{1,0:T(8,128)(4,1)S(1)} %copy.35), kind=kOutput, calls=%fused_computation.101 | convolution fusion | flops 404226048 | bytes 11534528 | tf_op jit(solution)/shard_map/inab,finb->fia/dot_general | solution.py:43
  410.9 57.7 %all-gather.3.cloned.1.call-done = f32[128,64,64]{2,1,0:T(8,128)} async-done(((f32[4,64,64]{2,1,0:T(8,128)}), f32[128,64,64]{2,1,0:T(8,128)}) %all-gather.3.cloned.1.call-update) | async-done | bytes 2097168 | tf_op jit(solution)/shard_map/all_gather | solution.py:91
  468.7 3.3 reduce_sum.9
  (424 shorter events, 257.3 us)
Async XLA Ops:
  7.2 461.5 %all-gather.3.cloned.1.call-start = ((), (), s32[]{:S(2)}) async-start(), calls=%async_computation | async-start | bytes 4325376 | tf_op jit(solution)/shard_map/all_gather | solution.py:91
  17.0 137.2 %collective-permute-start.15 = (bf16[64,2,128]{2,0,1:T(8,128)(2,1)}, bf16[64,2,128]{2,0,1:T(8,128)(2,1)}, u32[]{:S(2)}, u32[]{:S(2)}) collective-permute-start(bf16[64,2,128]{2,0,1:T(8,128)(2,1)} %select_bitcast_fusion.14), channel_id=1, source_target_pairs={{0,1},{1,0},{2,3},{3,2},{4,5},{5,4},{6,7},{7,6},{8,9},{9,8},{10,11... | collective-permute-start | bytes 98312 | tf_op jit(solution)/shard_map/ppermute | solution.py:14
  18.8 135.5 %collective-permute-start.16 = (bf16[2,128,128]{2,1,0:T(8,128)(2,1)}, bf16[2,128,128]{2,1,0:T(8,128)(2,1)S(1)}, u32[]{:S(2)}, u32[]{:S(2)}) collective-permute-start(bf16[2,128,128]{2,1,0:T(8,128)(2,1)} %get-tuple-element.19), channel_id=1, source_target_pairs={{0,1},{1,0},{2,3},{3,2},{4,5},{5,4},{6,7},{7,6},{8,9},{9,8},{10,11... | collective-permute-start | bytes 196616 | tf_op jit(solution)/shard_map/ppermute | solution.py:14
  20.1 137.7 %collective-permute-start.17 = (bf16[64,2,128]{2,0,1:T(8,128)(2,1)}, bf16[64,2,128]{2,0,1:T(8,128)(2,1)}, u32[]{:S(2)}, u32[]{:S(2)}) collective-permute-start(bf16[64,2,128]{2,0,1:T(8,128)(2,1)} %select_bitcast_fusion.13), channel_id=1, source_target_pairs={{0,2},{2,0},{1,3},{3,1},{4,6},{6,4},{5,7},{7,5},{8,10},{10,8},{9,1... | collective-permute-start | bytes 98312 | tf_op jit(solution)/shard_map/ppermute | solution.py:14
  23.1 134.8 %collective-permute-start.18 = (bf16[2,128,128]{2,1,0:T(8,128)(2,1)}, bf16[2,128,128]{2,1,0:T(8,128)(2,1)}, u32[]{:S(2)}, u32[]{:S(2)}) collective-permute-start(bf16[2,128,128]{2,1,0:T(8,128)(2,1)} %get-tuple-element.18), channel_id=1, source_target_pairs={{0,2},{2,0},{1,3},{3,1},{4,6},{6,4},{5,7},{7,5},{8,10},{10,8},{9,1... | collective-permute-start | bytes 196616 | tf_op jit(solution)/shard_map/ppermute | solution.py:14
  28.6 93.7 %collective-permute-start = (bf16[64,2,128]{2,0,1:T(8,128)(2,1)}, bf16[64,2,128]{2,0,1:T(8,128)(2,1)}, u32[]{:S(2)}, u32[]{:S(2)}) collective-permute-start(bf16[64,2,128]{2,0,1:T(8,128)(2,1)} %select_bitcast_fusion.29), channel_id=1, source_target_pairs={{0,1},{1,0},{2,3},{3,2},{4,5},{5,4},{6,7},{7,6},{8,9},{9,8},{10,11... | collective-permute-start | bytes 98312 | tf_op jit(solution)/shard_map/ppermute | solution.py:14
  140.0 22.5 %collective-permute-start.19 = (bf16[64,2,128]{2,0,1:T(8,128)(2,1)}, bf16[64,2,128]{2,0,1:T(8,128)(2,1)}, u32[]{:S(2)}, u32[]{:S(2)}) collective-permute-start(bf16[64,2,128]{2,0,1:T(8,128)(2,1)} %select_bitcast_fusion.12), channel_id=1, source_target_pairs={{0,4},{4,0},{1,5},{5,1},{2,6},{6,2},{3,7},{7,3},{8,12},{12,8},{9,1... | collective-permute-start | bytes 98312 | tf_op jit(solution)/shard_map/ppermute | solution.py:14
  157.9 13.8 %collective-permute-start.23 = (bf16[64,2,128]{2,0,1:T(8,128)(2,1)}, bf16[64,2,128]{2,0,1:T(8,128)(2,1)}, u32[]{:S(2)}, u32[]{:S(2)}) collective-permute-start(bf16[64,2,128]{2,0,1:T(8,128)(2,1)} %select_bitcast_fusion.10), channel_id=1, source_target_pairs={{0,16},{16,0},{1,17},{17,1},{2,18},{18,2},{3,19},{19,3},{4,20},{20... | collective-permute-start | bytes 98312 | tf_op jit(solution)/shard_map/ppermute | solution.py:14
  194.7 32.1 %collective-permute-start.25 = (bf16[64,2,128]{2,0,1:T(8,128)(2,1)}, bf16[64,2,128]{2,0,1:T(8,128)(2,1)}, u32[]{:S(2)}, u32[]{:S(2)}) collective-permute-start(bf16[64,2,128]{2,0,1:T(8,128)(2,1)} %select_bitcast_fusion.9), channel_id=1, source_target_pairs={{0,1},{1,0},{2,3},{3,2},{4,5},{5,4},{6,7},{7,6},{8,9},{9,8},{10,11... | collective-permute-start | bytes 98312 | tf_op jit(solution)/shard_map/ppermute | solution.py:14
  195.4 33.1 %collective-permute-start.26 = (bf16[64,2,128]{2,0,1:T(8,128)(2,1)}, bf16[64,2,128]{2,0,1:T(8,128)(2,1)}, u32[]{:S(2)}, u32[]{:S(2)}) collective-permute-start(bf16[64,2,128]{2,0,1:T(8,128)(2,1)} %select_bitcast_fusion.8), channel_id=1, source_target_pairs={{0,2},{2,0},{1,3},{3,1},{4,6},{6,4},{5,7},{7,5},{8,10},{10,8},{9,1... | collective-permute-start | bytes 98312 | tf_op jit(solution)/shard_map/ppermute | solution.py:14
  197.9 32.2 %collective-permute-start.27 = (bf16[64,2,128]{2,0,1:T(8,128)(2,1)}, bf16[64,2,128]{2,0,1:T(8,128)(2,1)}, u32[]{:S(2)}, u32[]{:S(2)}) collective-permute-start(bf16[64,2,128]{2,0,1:T(8,128)(2,1)} %select_bitcast_fusion.7), channel_id=1, source_target_pairs={{0,4},{4,0},{1,5},{5,1},{2,6},{6,2},{3,7},{7,3},{8,12},{12,8},{9,1... | collective-permute-start | bytes 98312 | tf_op jit(solution)/shard_map/ppermute | solution.py:14
  200.1 31.7 %collective-permute-start.28 = (bf16[64,2,128]{2,0,1:T(8,128)(2,1)}, bf16[64,2,128]{2,0,1:T(8,128)(2,1)}, u32[]{:S(2)}, u32[]{:S(2)}) collective-permute-start(bf16[64,2,128]{2,0,1:T(8,128)(2,1)} %select_bitcast_fusion.6), channel_id=1, source_target_pairs={{0,8},{8,0},{1,9},{9,1},{2,10},{10,2},{3,11},{11,3},{4,12},{12,4},... | collective-permute-start | bytes 98312 | tf_op jit(solution)/shard_map/ppermute | solution.py:14
  202.4 39.8 %collective-permute-start.29 = (bf16[64,2,128]{2,0,1:T(8,128)(2,1)}, bf16[64,2,128]{2,0,1:T(8,128)(2,1)}, u32[]{:S(2)}, u32[]{:S(2)}) collective-permute-start(bf16[64,2,128]{2,0,1:T(8,128)(2,1)} %select_bitcast_fusion.5), channel_id=1, source_target_pairs={{0,16},{16,0},{1,17},{17,1},{2,18},{18,2},{3,19},{19,3},{4,20},{20... | collective-permute-start | bytes 98312 | tf_op jit(solution)/shard_map/ppermute | solution.py:14
  283.3 35.5 %collective-permute-start.30 = (bf16[64,2,128]{2,0,1:T(8,128)(2,1)}, bf16[64,2,128]{2,0,1:T(8,128)(2,1)}, u32[]{:S(2)}, u32[]{:S(2)}) collective-permute-start(bf16[64,2,128]{2,0,1:T(8,128)(2,1)} %select_bitcast_fusion.4), channel_id=1, source_target_pairs={{0,1},{1,0},{2,3},{3,2},{4,5},{5,4},{6,7},{7,6},{8,9},{9,8},{10,11... | collective-permute-start | bytes 98312 | tf_op jit(solution)/shard_map/ppermute | solution.py:14
  284.0 36.4 %collective-permute-start.31 = (bf16[64,2,128]{2,0,1:T(8,128)(2,1)}, bf16[64,2,128]{2,0,1:T(8,128)(2,1)}, u32[]{:S(2)}, u32[]{:S(2)}) collective-permute-start(bf16[64,2,128]{2,0,1:T(8,128)(2,1)} %select_bitcast_fusion.3), channel_id=1, source_target_pairs={{0,2},{2,0},{1,3},{3,1},{4,6},{6,4},{5,7},{7,5},{8,10},{10,8},{9,1... | collective-permute-start | bytes 98312 | tf_op jit(solution)/shard_map/ppermute | solution.py:14
  285.1 38.2 %collective-permute-start.32 = (bf16[64,2,128]{2,0,1:T(8,128)(2,1)}, bf16[64,2,128]{2,0,1:T(8,128)(2,1)}, u32[]{:S(2)}, u32[]{:S(2)}) collective-permute-start(bf16[64,2,128]{2,0,1:T(8,128)(2,1)} %select_bitcast_fusion.2), channel_id=1, source_target_pairs={{0,4},{4,0},{1,5},{5,1},{2,6},{6,2},{3,7},{7,3},{8,12},{12,8},{9,1... | collective-permute-start | bytes 98312 | tf_op jit(solution)/shard_map/ppermute | solution.py:14
  286.3 40.1 %collective-permute-start.33 = (bf16[64,2,128]{2,0,1:T(8,128)(2,1)}, bf16[64,2,128]{2,0,1:T(8,128)(2,1)}, u32[]{:S(2)}, u32[]{:S(2)}) collective-permute-start(bf16[64,2,128]{2,0,1:T(8,128)(2,1)} %select_bitcast_fusion.1), channel_id=1, source_target_pairs={{0,8},{8,0},{1,9},{9,1},{2,10},{10,2},{3,11},{11,3},{4,12},{12,4},... | collective-permute-start | bytes 98312 | tf_op jit(solution)/shard_map/ppermute | solution.py:14
  287.2 42.4 %collective-permute-start.34 = (bf16[64,2,128]{2,0,1:T(8,128)(2,1)}, bf16[64,2,128]{2,0,1:T(8,128)(2,1)}, u32[]{:S(2)}, u32[]{:S(2)}) collective-permute-start(bf16[64,2,128]{2,0,1:T(8,128)(2,1)} %select_bitcast_fusion), channel_id=1, source_target_pairs={{0,16},{16,0},{1,17},{17,1},{2,18},{18,2},{3,19},{19,3},{4,20},{20... | collective-permute-start | bytes 98312 | tf_op jit(solution)/shard_map/ppermute | solution.py:14
  318.8 15.3 %collective-permute-start.5 = (bf16[64,2,128]{2,0,1:T(8,128)(2,1)}, bf16[64,2,128]{2,0,1:T(8,128)(2,1)S(1)}, u32[]{:S(2)}, u32[]{:S(2)}) collective-permute-start(bf16[64,2,128]{2,0,1:T(8,128)(2,1)} %select_bitcast_fusion.24), channel_id=1, source_target_pairs={{0,1},{1,0},{2,3},{3,2},{4,5},{5,4},{6,7},{7,6},{8,9},{9,8},{10,11... | collective-permute-start | bytes 98312 | tf_op jit(solution)/shard_map/ppermute | solution.py:14
  320.4 15.1 %collective-permute-start.6 = (bf16[64,2,128]{2,0,1:T(8,128)(2,1)}, bf16[64,2,128]{2,0,1:T(8,128)(2,1)S(1)}, u32[]{:S(2)}, u32[]{:S(2)}) collective-permute-start(bf16[64,2,128]{2,0,1:T(8,128)(2,1)} %select_bitcast_fusion.23), channel_id=1, source_target_pairs={{0,2},{2,0},{1,3},{3,1},{4,6},{6,4},{5,7},{7,5},{8,10},{10,8},{9,1... | collective-permute-start | bytes 98312 | tf_op jit(solution)/shard_map/ppermute | solution.py:14
  323.3 13.7 %collective-permute-start.7 = (bf16[64,2,128]{2,0,1:T(8,128)(2,1)}, bf16[64,2,128]{2,0,1:T(8,128)(2,1)S(1)}, u32[]{:S(2)}, u32[]{:S(2)}) collective-permute-start(bf16[64,2,128]{2,0,1:T(8,128)(2,1)} %select_bitcast_fusion.22), channel_id=1, source_target_pairs={{0,4},{4,0},{1,5},{5,1},{2,6},{6,2},{3,7},{7,3},{8,12},{12,8},{9,1... | collective-permute-start | bytes 98312 | tf_op jit(solution)/shard_map/ppermute | solution.py:14
  326.4 11.9 %collective-permute-start.8 = (bf16[64,2,128]{2,0,1:T(8,128)(2,1)}, bf16[64,2,128]{2,0,1:T(8,128)(2,1)S(1)}, u32[]{:S(2)}, u32[]{:S(2)}) collective-permute-start(bf16[64,2,128]{2,0,1:T(8,128)(2,1)} %select_bitcast_fusion.21), channel_id=1, source_target_pairs={{0,8},{8,0},{1,9},{9,1},{2,10},{10,2},{3,11},{11,3},{4,12},{12,4},... | collective-permute-start | bytes 98312 | tf_op jit(solution)/shard_map/ppermute | solution.py:14
  329.6 25.8 %collective-permute-start.9 = (bf16[64,2,128]{2,0,1:T(8,128)(2,1)}, bf16[64,2,128]{2,0,1:T(8,128)(2,1)}, u32[]{:S(2)}, u32[]{:S(2)}) collective-permute-start(bf16[64,2,128]{2,0,1:T(8,128)(2,1)} %select_bitcast_fusion.20), channel_id=1, source_target_pairs={{0,16},{16,0},{1,17},{17,1},{2,18},{18,2},{3,19},{19,3},{4,20},{20... | collective-permute-start | bytes 98312 | tf_op jit(solution)/shard_map/ppermute | solution.py:14
  382.8 14.7 %collective-permute-start.14 = (bf16[64,2,128]{2,0,1:T(8,128)(2,1)}, bf16[64,2,128]{2,0,1:T(8,128)(2,1)}, u32[]{:S(2)}, u32[]{:S(2)}) collective-permute-start(bf16[64,2,128]{2,0,1:T(8,128)(2,1)} %select_bitcast_fusion.15), channel_id=1, source_target_pairs={{0,16},{16,0},{1,17},{17,1},{2,18},{18,2},{3,19},{19,3},{4,20},{20... | collective-permute-start | bytes 98312 | tf_op jit(solution)/shard_map/ppermute | solution.py:14
  (97 other events, 844.5 us)
Sparse Core Ops, SparseCore 0:
  406.2 62.4 all-gather.2
